TPU v7x, 256 devices: a whole 4x4x8 slice. The times are simulated.
256 devices in a mesh: seq: 32 (over z_lo, x, core), cam: 4 (over y), tp: 2 (over z_hi).
Axes of the slice: x: 4, y: 4, z: 8 (z_hi: 2, z_lo: 4; z = z_hi * 4 + z_lo), core: 2. Of those that a mesh axis runs over, the one named last changes fastest.
Arguments:
- pixel_feature: bfloat16 [32768, 2048], P(('seq', 'cam'), 'tp'), may hold values from -6 to 6
- depth_score: float32 [32768, 59], P(('seq', 'cam')), may hold values from 0.05 to 5
- depth_bin: int32 [32768, 4], P(('seq', 'cam')), may hold values from 0 to 58
- cell_owner: int32 [131072, 1], P(('seq', 'cam')), may hold values from 0 to 31; in each aligned block of 1024 rows (0 to 1023, 1024 to 2047, ...) at most 64 rows name the same one
- cell_local: int32 [32768, 4], P(('seq', 'cam')), may hold values from 0 to 7
- frame_keep: int32 [64], replicated, may hold values 0 or 1
- norm_gain: float32 [2048], P('tp'), may hold values from 0.1 to 1.9
- w_query: bfloat16 [2048, 2048], P(None, ('cam', 'tp')), may hold values from -1.5 to 1.5
- w_key: bfloat16 [2048, 2048], P(None, ('cam', 'tp')), may hold values from -0.375 to 0.375
- w_value: bfloat16 [2048, 2048], P(None, ('cam', 'tp')), may hold values from -0.125 to 0.125
Outputs:
- attended: bfloat16 [16384, 2048], P('seq', ('cam', 'tp'))
Inputs may be any that keep to these rules, and one draw needn't show every extreme that they name: `cell_owner`: among the 1024 points of one index of seq and cam (aligned blocks of rows), no owner is named more than 64 times, a bound that some block reaches.
All inputs are finite; a program needn't handle non-finite values.
Results may differ from a plain program's by a relative error of at most 0.028.
The roundings to bfloat16 on the way count: a program that leaves them out, or rounds other values in their place, can miss the bound.
Values may be sent and summed in bfloat16 or wider, within the bound.
A program may use at most 64 MiB of HBM per device.

v0:
```python
import jax
import jax.numpy as jnp
from jax import lax
from jax.sharding import PartitionSpec as P

D = 2048
HD = 128
CELL_DEV = 8
epsilon = 1e-05
block_rows = 512


def attend(state, query, query_start, keys, values, key_start, frame_keep):
    frames = frame_keep.shape[0]
    frame_query = (query_start + jnp.arange(query.shape[0], dtype=jnp.int32)) % frames
    frame_key = (key_start + jnp.arange(keys.shape[0], dtype=jnp.int32)) % frames
    frame_list = jnp.arange(frames, dtype=jnp.int32)
    kept = jnp.sum(
        jnp.where(frame_key[:, None] == frame_list[None, :], frame_keep[None, :], 0), axis=1
    )
    allowed = (frame_key[None, :] <= frame_query[:, None]) & (
        (kept[None, :] > 0) | (frame_key[None, :] == frame_query[:, None])
    )
    scores = jnp.einsum("qhd,khd->hqk", query, keys, preferred_element_type=jnp.float32) * (
        1.0 / HD**0.5
    )
    accum, peak, total = state
    new_peak = jnp.maximum(peak, jnp.max(jnp.where(allowed[None], scores, -1e30), axis=2))
    factor = jnp.exp(peak - new_peak)
    expo = jnp.where(allowed[None], jnp.exp(scores - new_peak[:, :, None]), 0.0)
    mixed = jnp.einsum(
        "hqk,khd->hqd", expo.astype(jnp.bfloat16), values, preferred_element_type=jnp.float32
    )
    return (accum * factor[:, :, None] + mixed, new_peak, total * factor + jnp.sum(expo, axis=2))


def local(
    pixel_feature,
    depth_score,
    depth_bin,
    cell_owner,
    cell_local,
    frame_keep,
    norm_gain,
    w_query,
    w_key,
    w_value,
):
    pixels, half = pixel_feature.shape
    keep_count = depth_bin.shape[1]
    points = pixels * keep_count
    seq_count = lax.axis_size("seq")
    seq_index = lax.axis_index("seq")
    frames = frame_keep.shape[0]
    frames_dev = frames // seq_count
    tokens_dev = CELL_DEV * frames
    capacity = 2 * points // seq_count
    prob = depth_score / jnp.sum(depth_score, axis=1, keepdims=True)
    bins = jnp.arange(depth_score.shape[1], dtype=jnp.int32)
    picked = jnp.sum(
        jnp.where(depth_bin[:, :, None] == bins[None, None, :], prob[:, None, :], 0.0), axis=2
    )
    weight = picked.astype(jnp.bfloat16)
    point_index = jnp.arange(points, dtype=jnp.int32).reshape(pixels, keep_count)
    local_frame = point_index // (points // frames_dev)
    owner = cell_owner[:, 0].reshape(pixels, keep_count)
    owner_flat = owner.reshape(points)
    hits = (owner_flat[:, None] == jnp.arange(seq_count, dtype=jnp.int32)[None, :]).astype(
        jnp.int32
    )
    rank = jnp.sum(jnp.cumsum(hits, axis=0) * hits, axis=1) - 1
    slot = owner_flat * capacity + rank
    point_rows = jnp.repeat(pixel_feature, keep_count, axis=0)
    send_rows = jnp.zeros((seq_count * capacity, half), jnp.bfloat16).at[slot].set(point_rows)
    send_rows = send_rows.reshape(seq_count, capacity, half)
    frame_global = seq_index * frames_dev + local_frame
    describe = jnp.stack(
        [
            weight.reshape(points),
            cell_local.reshape(points).astype(jnp.bfloat16),
            frame_global.reshape(points).astype(jnp.bfloat16),
        ],
        axis=0,
    )
    send_meta = jnp.zeros((3, seq_count * capacity), jnp.bfloat16).at[:, slot].set(describe)
    send_meta = send_meta.reshape(3, seq_count, capacity).transpose(1, 0, 2)
    got_rows, got_meta = (
        lax.all_to_all(send_rows, "seq", split_axis=0, concat_axis=0, tiled=True),
        lax.all_to_all(send_meta, "seq", split_axis=0, concat_axis=0, tiled=True),
    )
    target = (
        got_meta[:, 1, :].astype(jnp.float32) * frames + got_meta[:, 2, :].astype(jnp.float32)
    ).reshape(-1)
    token_ids = jnp.arange(tokens_dev, dtype=jnp.float32)
    mixing = jnp.where(
        token_ids[:, None] == target[None, :], got_meta[:, 0, :].reshape(-1)[None, :], 0
    )
    pooled = jnp.dot(mixing, got_rows.reshape(-1, half), preferred_element_type=jnp.float32)
    bev = lax.psum(pooled, "cam")
    squares = lax.psum(jnp.sum(bev * bev, axis=1), "tp")
    normed = (bev * lax.rsqrt(squares[:, None] / D + epsilon) * norm_gain[None, :]).astype(
        jnp.bfloat16
    )
    width = w_query.shape[1]
    heads_dev = width // HD
    piece = lax.all_gather(normed, "tp", axis=1, tiled=True)
    query_sum = jnp.dot(piece, w_query, preferred_element_type=jnp.float32)
    key_sum = jnp.dot(piece, w_key, preferred_element_type=jnp.float32)
    value_sum = jnp.dot(piece, w_value, preferred_element_type=jnp.float32)
    query = query_sum.astype(jnp.bfloat16).reshape(tokens_dev, heads_dev, HD)
    keys = key_sum.astype(jnp.bfloat16).reshape(tokens_dev, heads_dev, HD)
    values = value_sum.astype(jnp.bfloat16).reshape(tokens_dev, heads_dev, HD)
    query_start = seq_index * tokens_dev
    start_state = (
        jnp.zeros((heads_dev, tokens_dev, HD), jnp.float32),
        jnp.full((heads_dev, tokens_dev), -1e30, jnp.float32),
        jnp.zeros((heads_dev, tokens_dev), jnp.float32),
    )
    piece_keys = lax.all_gather(keys, "seq", axis=0, tiled=True)
    piece_values = lax.all_gather(values, "seq", axis=0, tiled=True)
    count = piece_keys.shape[0]

    def one_block(index, inner):
        block_keys = lax.dynamic_slice_in_dim(piece_keys, index * block_rows, block_rows, 0)
        block_values = lax.dynamic_slice_in_dim(piece_values, index * block_rows, block_rows, 0)
        return attend(
            inner, query, query_start, block_keys, block_values, index * block_rows, frame_keep
        )

    accum, peak, total = lax.fori_loop(0, count // block_rows, one_block, start_state)
    result = accum / total[:, :, None]
    return result.transpose(1, 0, 2).reshape(tokens_dev, width).astype(jnp.bfloat16)


def solution(mesh):
    return jax.shard_map(
        local,
        mesh=mesh,
        in_specs=(
            P(("seq", "cam"), "tp"),
            P(("seq", "cam"), None),
            P(("seq", "cam"), None),
            P(("seq", "cam"), None),
            P(("seq", "cam"), None),
            P(),
            P("tp"),
            P(None, ("cam", "tp")),
            P(None, ("cam", "tp")),
            P(None, ("cam", "tp")),
        ),
        out_specs=P("seq", ("cam", "tp")),
        check_vma=False,
    )
```

profile of v0, /device:TPU:1, one launch (start us, length us, event | category | flops | bytes accessed | tf_op | source)
XLA Modules:
  0.0 587.0 jit_solution(16973022452448787255)
XLA Ops:
  11.1 9.0 %reduce-window.6 = s32[32,8,128]{2,1,0:T(8,128)S(1)} reduce-window(s32[32,8,128]{2,1,0:T(8,128)S(1)} %fusion.34, s32[]{:T(128)} %constant.143.clone.1), window={size=1x1x128 pad=0_0x0_0x127_0}, to_apply=%region_0.0 | reduce-window | flops 4161536 | bytes 262148 | tf_op jit(solution)/shard_map/reduce-window
  22.4 3.3 scatter_custom_fusion
  26.7 10.0 %all-to-all-start = ((bf16[32,3,64]{2,1,0:T(4,128)(2,1)}), bf16[32,3,64]{2,1,0:T(4,128)(2,1)S(1)}, u32[]{:S(2)}, u32[]{:S(2)}) async-start(bf16[32,3,64]{2,1,0:T(4,128)(2,1)} %bitcast.8), calls=%async_computation | async-start | bytes 65536 | tf_op jit(solution)/shard_map/all_to_all | solution.py:89
  36.7 1.7 broadcast_in_dim.171
  38.4 2.1 reshape.333
  40.4 8.6 %scatter_custom_fusion.1 = bf16[2048,1024]{1,0:T(8,128)(2,1)} fusion(s32[1024]{0:T(1024)S(1)} %bitcast.76, bf16[1024,1024]{1,0:T(8,128)(2,1)} %reshape.333, bf16[]{:T(256)} %constant.146.clone.1), kind=kCustom, calls=%fused_computation.44 | custom fusion | bytes 4194816 | tf_op jit(solution)/shard_map/scatter | solution.py:74
  49.0 7.8 %all-to-all-start.1 = ((bf16[32,64,1024]{2,1,0:T(8,128)(2,1)}), bf16[32,64,1024]{2,1,0:T(8,128)(2,1)}, u32[]{:S(2)}, u32[]{:S(2)}) async-start(bf16[32,64,1024]{2,1,0:T(8,128)(2,1)} %bitcast.65), calls=%async_computation.1 | async-start | bytes 8388608 | tf_op jit(solution)/shard_map/all_to_all | solution.py:88
  57.2 92.7 %all-to-all-done.1 = bf16[32,64,1024]{2,1,0:T(8,128)(2,1)} async-done(((bf16[32,64,1024]{2,1,0:T(8,128)(2,1)}), bf16[32,64,1024]{2,1,0:T(8,128)(2,1)}, u32[]{:S(2)}, u32[]{:S(2)}) %all-to-all-start.1) | async-done | bytes 4194336 | tf_op jit(solution)/shard_map/all_to_all | solution.py:88
  149.9 5.9 fusion.22
  155.8 64.2 %all-reduce.2.cloned.1.call-done = f32[512,1024]{1,0:T(8,128)} async-done(((f32[512,1024]{1,0:T(8,128)}), f32[512,1024]{1,0:T(8,128)}) %all-reduce.2.cloned.1.call-update) | async-done | bytes 2097168 | tf_op jit(solution)/shard_map/psum | solution.py:99
  220.0 2.0 multiply_reduce_fusion
  221.9 7.8 %psum.15 = f32[512]{0:T(512)S(1)} all-reduce(f32[512]{0:T(512)S(1)} %multiply_reduce_fusion), channel_id=1, replica_groups=mesh['seq'=32,'cam'=4,'tp'=2] {'tp'}, use_global_device_ids=true, to_apply=%region_9.10 | all-reduce | flops 512 | bytes 4096 | tf_op jit(solution)/shard_map/psum | solution.py:100
  231.2 65.9 %all-gather.4.cloned.1.call-done = bf16[512,2048]{1,0:T(8,128)(2,1)} async-done(((bf16[512,1024]{1,0:T(8,128)(2,1)}), bf16[512,2048]{1,0:T(8,128)(2,1)}) %all-gather.4.cloned.1.call-update) | async-done | bytes 2097168 | tf_op jit(solution)/shard_map/all_gather | solution.py:106
  297.2 2.5 convolution_convert_fusion
  300.6 2.0 convolution_convert_fusion.2
  303.5 2.6 convolution_convert_fusion.1
  306.3 59.7 %all-gather.8.cloned.1.call-done = bf16[16384,2,128]{2,0,1:T(8,128)(2,1)} async-done(((bf16[512,2,128]{2,0,1:T(8,128)(2,1)}), bf16[16384,2,128]{2,0,1:T(8,128)(2,1)}) %all-gather.8.cloned.1.call-update) | async-done | bytes 8388624 | tf_op jit(solution)/shard_map/all_gather | solution.py:120
  366.0 69.0 %all-gather.6.cloned.1.call-done = bf16[16384,2,128]{2,0,1:T(8,128)(2,1)} async-done(((bf16[512,2,128]{2,0,1:T(8,128)(2,1)}), bf16[16384,2,128]{2,0,1:T(8,128)(2,1)}) %all-gather.6.cloned.1.call-update) | async-done | bytes 8388624 | tf_op jit(solution)/shard_map/all_gather | solution.py:119
  435.0 144.5 %while.20 = (s32[]{:T(128)}, f32[2,512,128]{2,1,0:T(8,128)S(1)}, f32[2,512]{1,0:T(2,128)S(1)}, f32[2,512]{1,0:T(2,128)S(1)}, s32[]{:T(128)}, /*index=5*/s32[64]{...) while((s32[]{:T(128)}, f32[2,512,128]{2,1,0:T(8,128)S(1)}, ...), condition=%wide.region_14.15_spmd.clone, body=%wide.region_10.14_spmd.clone.sunk | while | flops 275760128 | bytes 9256399 | solution.py:130
  437.5 2.0 convolution_add_fusion.2
  439.9 1.5 fusion.58
  442.0 2.0 convolution_add_fusion.2
  446.5 2.0 convolution_add_fusion.2
  451.0 2.0 convolution_add_fusion.2
  455.5 2.0 convolution_add_fusion.2
  458.0 1.5 fusion.58
  460.1 2.0 convolution_add_fusion.2
  464.6 2.0 convolution_add_fusion.2
  469.1 2.0 convolution_add_fusion.2
  473.6 2.0 convolution_add_fusion.2
  476.1 1.5 fusion.58
  478.1 2.0 convolution_add_fusion.2
  482.7 2.0 convolution_add_fusion.2
  485.1 1.5 fusion.58
  487.2 2.0 convolution_add_fusion.2
  491.7 2.0 convolution_add_fusion.2
  494.2 1.5 fusion.58
  496.2 2.0 convolution_add_fusion.2
  500.7 2.0 convolution_add_fusion.2
  503.2 1.5 fusion.58
  505.2 2.0 convolution_add_fusion.2
  507.7 1.5 fusion.58
  509.8 2.0 convolution_add_fusion.2
  512.2 1.5 fusion.58
  514.3 2.0 convolution_add_fusion.2
  518.8 2.0 convolution_add_fusion.2
  521.3 1.5 fusion.58
  523.3 2.0 convolution_add_fusion.2
  525.8 1.5 fusion.58
  527.8 2.0 convolution_add_fusion.2
  530.3 1.5 fusion.58
  532.4 2.0 convolution_add_fusion.2
  536.9 2.0 convolution_add_fusion.2
  541.4 2.0 convolution_add_fusion.2
  545.9 2.0 convolution_add_fusion.2
  548.4 1.5 fusion.58
  550.4 2.0 convolution_add_fusion.2
  554.9 2.0 convolution_add_fusion.2
  559.5 2.0 convolution_add_fusion.2
  564.0 2.0 convolution_add_fusion.2
  566.4 1.5 fusion.58
  568.5 2.0 convolution_add_fusion.2
  573.0 2.0 convolution_add_fusion.2
  577.5 2.0 convolution_add_fusion.2
  (331 shorter events, 72.7 us)
Async XLA Ops:
  6.5 290.6 %copy-start = (bf16[2048,256]{1,0:T(8,128)(2,1)S(1)}, bf16[2048,256]{1,0:T(8,128)(2,1)}, u32[]{:S(2)}) copy-start(bf16[2048,256]{1,0:T(8,128)(2,1)} %param.21) | copy-start | bytes 3145732
  26.7 22.4 %all-to-all-start = ((bf16[32,3,64]{2,1,0:T(4,128)(2,1)}), bf16[32,3,64]{2,1,0:T(4,128)(2,1)S(1)}, u32[]{:S(2)}, u32[]{:S(2)}) async-start(bf16[32,3,64]{2,1,0:T(4,128)(2,1)} %bitcast.8), calls=%async_computation | async-start | bytes 65536 | tf_op jit(solution)/shard_map/all_to_all | solution.py:89
  49.0 100.9 %all-to-all-start.1 = ((bf16[32,64,1024]{2,1,0:T(8,128)(2,1)}), bf16[32,64,1024]{2,1,0:T(8,128)(2,1)}, u32[]{:S(2)}, u32[]{:S(2)}) async-start(bf16[32,64,1024]{2,1,0:T(8,128)(2,1)} %bitcast.65), calls=%async_computation.1 | async-start | bytes 8388608 | tf_op jit(solution)/shard_map/all_to_all | solution.py:88
  56.8 163.2 %all-reduce.2.cloned.1.call-start = ((), (), s32[]{:S(2)}) async-start(), calls=%async_computation.2 | async-start | bytes 4194304 | tf_op jit(solution)/shard_map/psum | solution.py:99
  155.7 74.0 %copy-start.3 = (f32[1024]{0:T(1024)S(1)}, f32[1024]{0:T(1024)}, u32[]{:S(2)}) copy-start(f32[1024]{0:T(1024)} %param.18) | copy-start | bytes 12292
  155.8 141.4 %all-gather.4.cloned.1.call-start = ((), (), s32[]{:S(2)}) async-start(), calls=%async_computation.3 | async-start | bytes 3145728 | tf_op jit(solution)/shard_map/all_gather | solution.py:106
  220.0 9.7 %copy-start.1 = (f32[512,1024]{1,0:T(8,128)S(1)}, f32[512,1024]{1,0:T(8,128)}, u32[]{:S(2)}) copy-start(f32[512,1024]{1,0:T(8,128)} %all-reduce.2.cloned.1.call-done) | copy-start | bytes 6291460
  231.0 135.0 %all-gather.8.cloned.1.call-start = ((), (), s32[]{:S(2)}) async-start(), calls=%async_computation.5 | async-start | bytes 8650752 | tf_op jit(solution)/shard_map/all_gather | solution.py:120
  297.2 3.4 copy-start.4
  300.5 134.4 %all-gather.6.cloned.1.call-start = ((), (), s32[]{:S(2)}) async-start(), calls=%async_computation.4 | async-start | bytes 8650752 | tf_op jit(solution)/shard_map/all_gather | solution.py:119
  303.5 131.5 %copy-start.2 = (s32[64]{0:T(128)S(1)}, s32[64]{0:T(128)}, u32[]{:S(2)}) copy-start(s32[64]{0:T(128)} %param.17) | copy-start | bytes 772
Sparse Core Ops, SparseCore 0:
  155.9 64.0 all-reduce.1
  231.1 66.0 all-gather.3
  300.7 65.2 all-gather.7
  367.7 67.1 all-gather.5
where the time goes:
time: 590 us; the launch traced here: 587 us
  waiting for transfers between devices  352 us (60%)
  matrix products  124 us (21%)
  other arithmetic  50.4 us (9%)
  local copies, waits for them, and re-layouts  19.9 us (3%)
  starting transfers between devices  18.1 us (3%)
  between operations  13.3 us (2%)
  blocking collectives  7.76 us (1%)
    all_to_all x1, waiting for transfers between devices, local(): lax.all_to_all(send_rows, 'seq', split_axis=0, concat_axis=0, tiled=True)  92.7 us
    all_gather x1, waiting for transfers between devices, local(): piece_keys = lax.all_gather(keys, 'seq', axis=0, tiled=True)  69 us
    all_gather x1, waiting for transfers between devices, local(): piece = lax.all_gather(normed, 'tp', axis=1, tiled=True)  65.9 us
    psum x1, waiting for transfers between devices, local(): bev = lax.psum(pooled, 'cam')  64.2 us
    dot_general x32, matrix products, attend(): jnp.einsum('hqk,khd->hqd', expo.astype(jnp.bfloat16), values, preferred_e...  62.6 us
    all_gather x1, waiting for transfers between devices, local(): piece_values = lax.all_gather(values, 'seq', axis=0, tiled=True)  59.7 us
    dot_general x32, matrix products, attend(): jnp.einsum('qhd,khd->hqk', query, keys, preferred_element_type=jnp.float32)  48.2 us
    reduce_sum x32, other arithmetic, attend(): jnp.sum(expo, axis=2)  15.9 us
  transfers between devices with their start and end apart: 6, of which 5 were waited for; matrix products, arithmetic and copies ran while one was open for 3% of the time, Pallas kernels for 0%

commit v1 on v0

--- a/solution.py
+++ b/solution.py
@@ -96,7 +96,7 @@
         token_ids[:, None] == target[None, :], got_meta[:, 0, :].reshape(-1)[None, :], 0
     )
     pooled = jnp.dot(mixing, got_rows.reshape(-1, half), preferred_element_type=jnp.float32)
-    bev = lax.psum(pooled, "cam")
+    bev = jnp.sum(lax.all_gather(pooled, "cam"), axis=0)
     squares = lax.psum(jnp.sum(bev * bev, axis=1), "tp")
     normed = (bev * lax.rsqrt(squares[:, None] / D + epsilon) * norm_gain[None, :]).astype(
         jnp.bfloat16

time: 590 us -> 615 us (1.042)
  waiting for transfers between devices: 352 us -> 375 us
    all_gather x0 -> x1, waiting for transfers between devices: none -> 85.8 us  [local(): bev = jnp.sum(lax.all_gather(pooled, 'cam'), axis=0)]
    psum x1 -> x0, waiting for transfers between devices: 64.2 us -> none  [local(): bev = lax.psum(pooled, 'cam')]
where the time goes in v1:
time: 615 us; the launch traced here: 613 us
  waiting for transfers between devices  375 us (61%)
  matrix products  124 us (20%)
  other arithmetic  53.2 us (9%)
  local copies, waits for them, and re-layouts  19.9 us (3%)
  starting transfers between devices  18.1 us (3%)
  between operations  13.3 us (2%)
  blocking collectives  7.76 us (1%)
    all_to_all x1, waiting for transfers between devices, local(): lax.all_to_all(send_rows, 'seq', split_axis=0, concat_axis=0, tiled=True)  92.7 us
    all_gather x1, waiting for transfers between devices, local(): bev = jnp.sum(lax.all_gather(pooled, 'cam'), axis=0)  85.8 us
    all_gather x1, waiting for transfers between devices, local(): piece_keys = lax.all_gather(keys, 'seq', axis=0, tiled=True)  69 us
    all_gather x1, waiting for transfers between devices, local(): piece = lax.all_gather(normed, 'tp', axis=1, tiled=True)  67.3 us
    dot_general x32, matrix products, attend(): jnp.einsum('hqk,khd->hqd', expo.astype(jnp.bfloat16), values, preferred_e...  62.6 us
    all_gather x1, waiting for transfers between devices, local(): piece_values = lax.all_gather(values, 'seq', axis=0, tiled=True)  59.7 us
    dot_general x32, matrix products, attend(): jnp.einsum('qhd,khd->hqk', query, keys, preferred_element_type=jnp.float32)  48.2 us
    reduce_sum x32, other arithmetic, attend(): jnp.sum(expo, axis=2)  15.9 us
  transfers between devices with their start and end apart: 6, of which 5 were waited for; matrix products, arithmetic and copies ran while one was open for 3% of the time, Pallas kernels for 0%

profile of v1, /device:TPU:1, one launch (start us, length us, event | category | flops | bytes accessed | tf_op | source)
XLA Modules:
  0.0 612.9 jit_solution(9555049285022522366)
XLA Ops:
  11.1 9.0 %reduce-window.6 = s32[32,8,128]{2,1,0:T(8,128)S(1)} reduce-window(s32[32,8,128]{2,1,0:T(8,128)S(1)} %fusion.34, s32[]{:T(128)} %constant.143.clone.1), window={size=1x1x128 pad=0_0x0_0x127_0}, to_apply=%region_0.0 | reduce-window | flops 4161536 | bytes 262148 | tf_op jit(solution)/shard_map/reduce-window
  22.4 3.3 scatter_custom_fusion
  26.7 10.0 %all-to-all-start = ((bf16[32,3,64]{2,1,0:T(4,128)(2,1)}), bf16[32,3,64]{2,1,0:T(4,128)(2,1)S(1)}, u32[]{:S(2)}, u32[]{:S(2)}) async-start(bf16[32,3,64]{2,1,0:T(4,128)(2,1)} %bitcast.8), calls=%async_computation | async-start | bytes 65536 | tf_op jit(solution)/shard_map/all_to_all | solution.py:89
  36.7 1.7 broadcast_in_dim.171
  38.4 2.1 reshape.333
  40.4 8.6 %scatter_custom_fusion.1 = bf16[2048,1024]{1,0:T(8,128)(2,1)} fusion(s32[1024]{0:T(1024)S(1)} %bitcast.78, bf16[1024,1024]{1,0:T(8,128)(2,1)} %reshape.333, bf16[]{:T(256)} %constant.146.clone.1), kind=kCustom, calls=%fused_computation.44 | custom fusion | bytes 4194816 | tf_op jit(solution)/shard_map/scatter | solution.py:74
  49.0 7.8 %all-to-all-start.1 = ((bf16[32,64,1024]{2,1,0:T(8,128)(2,1)}), bf16[32,64,1024]{2,1,0:T(8,128)(2,1)}, u32[]{:S(2)}, u32[]{:S(2)}) async-start(bf16[32,64,1024]{2,1,0:T(8,128)(2,1)} %bitcast.66), calls=%async_computation.1 | async-start | bytes 8388608 | tf_op jit(solution)/shard_map/all_to_all | solution.py:88
  57.2 92.7 %all-to-all-done.1 = bf16[32,64,1024]{2,1,0:T(8,128)(2,1)} async-done(((bf16[32,64,1024]{2,1,0:T(8,128)(2,1)}), bf16[32,64,1024]{2,1,0:T(8,128)(2,1)}, u32[]{:S(2)}, u32[]{:S(2)}) %all-to-all-start.1) | async-done | bytes 4194336 | tf_op jit(solution)/shard_map/all_to_all | solution.py:88
  149.9 5.9 fusion.22
  156.1 85.8 %all-gather.12.cloned.1.call-done = f32[2048,1024]{1,0:T(8,128)} async-done(((f32[512,1024]{1,0:T(8,128)}), f32[2048,1024]{1,0:T(8,128)}) %all-gather.12.cloned.1.call-update) | async-done | bytes 8388624 | tf_op jit(solution)/shard_map/all_gather | solution.py:99
  241.9 4.6 reduce_sum.80
  246.7 7.8 %psum.7 = f32[512]{0:T(512)S(1)} all-reduce(f32[512]{0:T(512)S(1)} %multiply_reduce_fusion), channel_id=1, replica_groups=mesh['seq'=32,'cam'=4,'tp'=2] {'tp'}, use_global_device_ids=true, to_apply=%region_9.10 | all-reduce | flops 512 | bytes 4096 | tf_op jit(solution)/shard_map/psum | solution.py:100
  255.8 67.3 %all-gather.6.cloned.1.call-done = bf16[512,2048]{1,0:T(8,128)(2,1)} async-done(((bf16[512,1024]{1,0:T(8,128)(2,1)}), bf16[512,2048]{1,0:T(8,128)(2,1)}) %all-gather.6.cloned.1.call-update) | async-done | bytes 2097168 | tf_op jit(solution)/shard_map/all_gather | solution.py:106
  323.1 2.5 convolution_convert_fusion
  326.5 2.0 convolution_convert_fusion.2
  329.4 2.6 convolution_convert_fusion.1
  332.2 59.7 %all-gather.10.cloned.1.call-done = bf16[16384,2,128]{2,0,1:T(8,128)(2,1)} async-done(((bf16[512,2,128]{2,0,1:T(8,128)(2,1)}), bf16[16384,2,128]{2,0,1:T(8,128)(2,1)}) %all-gather.10.cloned.1.call-update) | async-done | bytes 8388624 | tf_op jit(solution)/shard_map/all_gather | solution.py:120
  391.9 69.0 %all-gather.8.cloned.1.call-done = bf16[16384,2,128]{2,0,1:T(8,128)(2,1)} async-done(((bf16[512,2,128]{2,0,1:T(8,128)(2,1)}), bf16[16384,2,128]{2,0,1:T(8,128)(2,1)}) %all-gather.8.cloned.1.call-update) | async-done | bytes 8388624 | tf_op jit(solution)/shard_map/all_gather | solution.py:119
  460.9 144.5 %while.20 = (s32[]{:T(128)}, f32[2,512,128]{2,1,0:T(8,128)S(1)}, f32[2,512]{1,0:T(2,128)S(1)}, f32[2,512]{1,0:T(2,128)S(1)}, s32[]{:T(128)}, /*index=5*/s32[64]{...) while((s32[]{:T(128)}, f32[2,512,128]{2,1,0:T(8,128)S(1)}, ...), condition=%wide.region_14.15_spmd.clone, body=%wide.region_10.14_spmd.clone.sunk | while | flops 275760128 | bytes 9256399 | solution.py:130
  461.3 1.5 fusion.58
  463.4 2.0 convolution_add_fusion.2
  465.8 1.5 fusion.58
  467.9 2.0 convolution_add_fusion.2
  472.4 2.0 convolution_add_fusion.2
  474.9 1.5 fusion.58
  476.9 2.0 convolution_add_fusion.2
  479.4 1.5 fusion.58
  481.4 2.0 convolution_add_fusion.2
  483.9 1.5 fusion.58
  486.0 2.0 convolution_add_fusion.2
  490.5 2.0 convolution_add_fusion.2
  492.9 1.5 fusion.58
  495.0 2.0 convolution_add_fusion.2
  497.5 1.5 fusion.58
  499.5 2.0 convolution_add_fusion.2
  502.0 1.5 fusion.58
  504.0 2.0 convolution_add_fusion.2
  508.5 2.0 convolution_add_fusion.2
  513.1 2.0 convolution_add_fusion.2
  517.6 2.0 convolution_add_fusion.2
  520.1 1.5 fusion.58
  522.1 2.0 convolution_add_fusion.2
  526.6 2.0 convolution_add_fusion.2
  531.1 2.0 convolution_add_fusion.2
  535.7 2.0 convolution_add_fusion.2
  538.1 1.5 fusion.58
  540.2 2.0 convolution_add_fusion.2
  544.7 2.0 convolution_add_fusion.2
  549.2 2.0 convolution_add_fusion.2
  553.7 2.0 convolution_add_fusion.2
  556.2 1.5 fusion.58
  558.2 2.0 convolution_add_fusion.2
  562.8 2.0 convolution_add_fusion.2
  567.3 2.0 convolution_add_fusion.2
  571.8 2.0 convolution_add_fusion.2
  574.3 1.5 fusion.58
  576.3 2.0 convolution_add_fusion.2
  580.8 2.0 convolution_add_fusion.2
  585.4 2.0 convolution_add_fusion.2
  589.9 2.0 convolution_add_fusion.2
  592.3 1.5 fusion.58
  594.4 2.0 convolution_add_fusion.2
  598.9 2.0 convolution_add_fusion.2
  603.4 2.0 convolution_add_fusion.2
  (330 shorter events, 72.9 us)
Async XLA Ops:
  6.5 316.5 %copy-start = (bf16[2048,256]{1,0:T(8,128)(2,1)S(1)}, bf16[2048,256]{1,0:T(8,128)(2,1)}, u32[]{:S(2)}) copy-start(bf16[2048,256]{1,0:T(8,128)(2,1)} %param.21) | copy-start | bytes 3145732
  26.7 22.4 %all-to-all-start = ((bf16[32,3,64]{2,1,0:T(4,128)(2,1)}), bf16[32,3,64]{2,1,0:T(4,128)(2,1)S(1)}, u32[]{:S(2)}, u32[]{:S(2)}) async-start(bf16[32,3,64]{2,1,0:T(4,128)(2,1)} %bitcast.8), calls=%async_computation | async-start | bytes 65536 | tf_op jit(solution)/shard_map/all_to_all | solution.py:89
  49.0 100.9 %all-to-all-start.1 = ((bf16[32,64,1024]{2,1,0:T(8,128)(2,1)}), bf16[32,64,1024]{2,1,0:T(8,128)(2,1)}, u32[]{:S(2)}, u32[]{:S(2)}) async-start(bf16[32,64,1024]{2,1,0:T(8,128)(2,1)} %bitcast.66), calls=%async_computation.1 | async-start | bytes 8388608 | tf_op jit(solution)/shard_map/all_to_all | solution.py:88
  56.8 185.1 %all-gather.12.cloned.1.call-start = ((), (), s32[]{:S(2)}) async-start(), calls=%async_computation.5 | async-start | bytes 10485760 | tf_op jit(solution)/shard_map/all_gather | solution.py:99
  155.8 167.2 %all-gather.6.cloned.1.call-start = ((), (), s32[]{:S(2)}) async-start(), calls=%async_computation.2 | async-start | bytes 3145728 | tf_op jit(solution)/shard_map/all_gather | solution.py:106
  246.5 8.0 %copy-start.2 = (f32[1024]{0:T(1024)S(1)}, f32[1024]{0:T(1024)}, u32[]{:S(2)}) copy-start(f32[1024]{0:T(1024)} %param.18) | copy-start | bytes 12292
  255.7 136.2 %all-gather.10.cloned.1.call-start = ((), (), s32[]{:S(2)}) async-start(), calls=%async_computation.4 | async-start | bytes 8650752 | tf_op jit(solution)/shard_map/all_gather | solution.py:120
  323.1 3.4 copy-start.3
  326.4 134.4 %all-gather.8.cloned.1.call-start = ((), (), s32[]{:S(2)}) async-start(), calls=%async_computation.3 | async-start | bytes 8650752 | tf_op jit(solution)/shard_map/all_gather | solution.py:119
  329.4 131.5 %copy-start.1 = (s32[64]{0:T(128)S(1)}, s32[64]{0:T(128)}, u32[]{:S(2)}) copy-start(s32[64]{0:T(128)} %param.17) | copy-start | bytes 772
Sparse Core Ops, SparseCore 0:
  156.0 85.8 all-gather.11
  255.8 67.1 all-gather.5
  326.6 65.2 all-gather.9
  393.6 67.1 all-gather.7
